TPU v7x, 128 devices: a whole 4x4x4 slice. The times are simulated.
128 devices in a mesh: dp: 64 (over z, y, x), tensor: 2 (over core).
Axes of the slice: x: 4, y: 4, z: 4, core: 2. Of those that a mesh axis runs over, the one named last changes fastest.
Arguments:
- square_grad: float32 [32, 2359296], P(None, ('dp', 'tensor')), may hold values from -80 to 80
- square_state: float32 [32, 2359296], P(None, ('dp', 'tensor')), may hold values from -6 to 6
- swiglu_grad: float32 [24, 6291456], P(None, ('dp', 'tensor')), may hold values from -80 to 80
- swiglu_state: float32 [24, 6291456], P(None, ('dp', 'tensor')), may hold values from -6 to 6
- square_order: int32 [32], replicated, may hold values from 0 to 31, each once
- swiglu_order: int32 [24], replicated, may hold values from 0 to 23, each once
- owners: int32 [56], replicated, may hold values from 0 to 63, as said below
- vector_values: float32 [172032], P(('dp', 'tensor')), may hold values from -6 to 6
- vector_grad: float32 [172032], P(('dp', 'tensor')), may hold values from -6 to 6
- vector_first: float32 [172032], P(('dp', 'tensor')), may hold values from -4 to 4
- vector_second: float32 [172032], P(('dp', 'tensor')), may hold values from 0.01 to 1
- embed_values: float32 [8192, 1536], P('dp', 'tensor'), may hold values from -6 to 6
- embed_grad: float32 [8192, 1536], P('dp', 'tensor'), may hold values from -6 to 6
- embed_first: float32 [8192, 1536], P('dp', 'tensor'), may hold values from -4 to 4
- embed_second: float32 [8192, 1536], P('dp', 'tensor'), may hold values from 0.01 to 1
- embed_ranges: int32 [16, 2], replicated, may hold values from 0 to 8192, as said below
Outputs:
- square_next: float32 [32, 2359296], P(None, ('dp', 'tensor'))
- swiglu_next: float32 [24, 6291456], P(None, ('dp', 'tensor'))
- square_update: bfloat16 [32, 1536, 1536], P(None, 'dp', 'tensor')
- swiglu_update: bfloat16 [24, 1536, 4096], P(None, 'dp', 'tensor')
- owner_norms: float32 [64], P('dp')
- vector_step: float32 [172032], P(('dp', 'tensor'))
- first_vector: float32 [172032], P(('dp', 'tensor'))
- second_vector: float32 [172032], P(('dp', 'tensor'))
- embed_step: float32 [8192, 1536], P('dp', 'tensor')
- first_embed: float32 [8192, 1536], P('dp', 'tensor')
- second_embed: float32 [8192, 1536], P('dp', 'tensor')
Inputs may be any that keep to these rules, and one draw needn't show every extreme that they name: Different matrices have different owners. `square_order`: each matrix once. `swiglu_order`: each matrix once. `embed_ranges`: start < end in every row.
All inputs are finite; a program needn't handle non-finite values.
Results may differ from a plain program's by a relative error of at most 0.0065.
Values may be sent and summed in bfloat16 or wider, within the bound.
A program may use at most 128 MiB of HBM per device.

v0:
```python
import math
import jax
import jax.numpy as jnp
from jax import lax
from jax.sharding import PartitionSpec as P

D = 1536
FF = 4096
NS_STEPS = 2
QUINTIC_LINEAR = 3.4445
QUINTIC_CUBIC = -4.775
QUINTIC_FIFTH = 2.0315
MOMENTUM = 0.95
BIAS_FIRST = 1.0 - 0.9**10
BIAS_SECOND = 1.0 - 0.95**10


def momentum_terms(gradient, state):
    state_next = MOMENTUM * state + gradient
    return (state_next, (gradient + MOMENTUM * state_next).astype(jnp.bfloat16))


def adamw_terms(values, gradient, first, second):
    first_next = 0.9 * first + 0.1 * gradient
    second_next = 0.95 * second + 0.05 * gradient * gradient
    direction = (
        first_next / BIAS_FIRST / (jnp.sqrt(second_next / BIAS_SECOND) + 1e-08) + 0.1 * values
    )
    return (direction, first_next, second_next)


def table_lookup(table, positions):
    matches = positions[:, None] == jnp.arange(table.shape[0], dtype=jnp.int32)[None, :]
    return jnp.sum(jnp.where(matches, table[None, :], 0), axis=1)


def select_pieces(pieces, piece_owner, targets):
    matched = piece_owner[None, :] == targets[:, None]
    chosen = jnp.sum(
        jnp.where(matched, jnp.arange(piece_owner.shape[0], dtype=jnp.int32)[None, :], 0), axis=1
    )
    present = jnp.any(matched, axis=1)
    picked = jnp.where(present[:, None, None, None], pieces[chosen], jnp.zeros((), jnp.bfloat16))
    return (picked, chosen, present)


def local(
    square_grad,
    square_state,
    swiglu_grad,
    swiglu_state,
    square_order,
    swiglu_order,
    owners,
    vector_values,
    vector_grad,
    vector_first,
    vector_second,
    embed_values,
    embed_grad,
    embed_first,
    embed_second,
    embed_ranges,
):
    wide_count = lax.axis_size("dp")
    split_count = lax.axis_size("tensor")
    wide_index = lax.axis_index("dp")
    square_count = square_grad.shape[0]
    swiglu_count = swiglu_grad.shape[0]
    flat_rows = D // (wide_count * split_count)
    slot_width = FF // split_count
    square_width = D // split_count
    square_next, square_send = momentum_terms(square_grad, square_state)
    swiglu_next, swiglu_send = momentum_terms(swiglu_grad, swiglu_state)
    square_pieces = square_send.reshape(
        square_count, flat_rows, split_count, square_width
    ).transpose(0, 2, 1, 3)
    swiglu_pieces = swiglu_send.reshape(swiglu_count, flat_rows, split_count, slot_width).transpose(
        0, 2, 1, 3
    )
    square_owner = table_lookup(owners[:square_count], square_order)
    swiglu_owner = table_lookup(owners[square_count:], swiglu_order)
    targets = jnp.arange(wide_count, dtype=jnp.int32)
    square_mine = jnp.any(square_owner == wide_index)
    owned = square_mine | jnp.any(swiglu_owner == wide_index)
    factor = jnp.where(square_mine, jnp.float32(math.sqrt(D)), jnp.float32(math.sqrt(FF)))
    widened = jnp.pad(square_pieces, ((0, 0), (0, 0), (0, 0), (0, slot_width - square_width)))
    all_pieces = jnp.concatenate([widened, swiglu_pieces], axis=0)
    slot_owner = jnp.concatenate([square_owner, swiglu_owner])
    outgoing, chosen, present = select_pieces(all_pieces, slot_owner, targets)
    arrived = lax.all_to_all(
        outgoing.reshape(D, slot_width), ("dp", "tensor"), split_axis=0, concat_axis=0, tiled=True
    )
    iterate = arrived
    first_scale = jnp.float32(1.0)
    for round_index in range(NS_STEPS):
        current = iterate
        gram_part = lax.psum_scatter(
            jnp.einsum("rc,sc->rs", current, current, preferred_element_type=jnp.float32),
            "tensor",
            scatter_dimension=0,
            tiled=True,
        )
        if round_index == 0:
            squares_total = lax.psum(jnp.sum(gram_part * gram_part), "tensor")
            gram_scale = jnp.sqrt(squares_total) + 1e-06
            first_scale = gram_scale
        else:
            gram_scale = jnp.float32(1.0)
        normed_part = (gram_part / gram_scale).astype(jnp.bfloat16)
        squared = jnp.dot(
            normed_part,
            lax.all_gather(normed_part, "tensor", axis=0, tiled=True),
            preferred_element_type=jnp.float32,
        )
        polynomial = (
            QUINTIC_CUBIC * normed_part.astype(jnp.float32) + QUINTIC_FIFTH * squared
        ).astype(jnp.bfloat16)
        product = jnp.dot(
            lax.all_gather(polynomial, "tensor", axis=0, tiled=True),
            current,
            preferred_element_type=jnp.float32,
        )
        mixed = (QUINTIC_LINEAR * current.astype(jnp.float32) + product) / jnp.sqrt(gram_scale)
        if round_index == NS_STEPS - 1:
            iterate = (factor * mixed).astype(jnp.bfloat16)
        else:
            iterate = mixed.astype(jnp.bfloat16)
    returned = lax.all_to_all(
        iterate.reshape(wide_count, D // wide_count, slot_width),
        "dp",
        split_axis=0,
        concat_axis=0,
        tiled=True,
    )
    square_update = returned[owners[:square_count]][:, :, :square_width]
    swiglu_update = returned[owners[square_count:]]
    owner_norms = jnp.where(owned, 0.5 * jnp.log(first_scale), 0.0).reshape(1)
    vector_step, first_vector, second_vector = adamw_terms(
        vector_values, vector_grad, vector_first, vector_second
    )
    embed_rows = embed_values.shape[0]
    row_numbers = wide_index * embed_rows + jnp.arange(embed_rows, dtype=jnp.int32)
    inside = (row_numbers[:, None] >= embed_ranges[None, :, 0]) & (
        row_numbers[:, None] < embed_ranges[None, :, 1]
    )
    row_live = jnp.sum(inside.astype(jnp.int32), axis=1) > 0
    direction, first_next, second_next = adamw_terms(
        embed_values, embed_grad, embed_first, embed_second
    )
    embed_step = jnp.where(row_live[:, None], direction, 0.0)
    first_embed = jnp.where(row_live[:, None], first_next, embed_first)
    second_embed = jnp.where(row_live[:, None], second_next, embed_second)
    return (
        square_next,
        swiglu_next,
        square_update,
        swiglu_update,
        owner_norms,
        vector_step,
        first_vector,
        second_vector,
        embed_step,
        first_embed,
        second_embed,
    )


def solution(mesh):
    placed = (
        P(None, ("dp", "tensor")),
        P(None, ("dp", "tensor")),
        P(None, ("dp", "tensor")),
        P(None, ("dp", "tensor")),
        P(),
        P(),
        P(),
        P(("dp", "tensor")),
        P(("dp", "tensor")),
        P(("dp", "tensor")),
        P(("dp", "tensor")),
        P("dp", "tensor"),
        P("dp", "tensor"),
        P("dp", "tensor"),
        P("dp", "tensor"),
        P(),
    )
    return jax.shard_map(
        local,
        mesh=mesh,
        in_specs=placed,
        out_specs=(
            P(None, ("dp", "tensor")),
            P(None, ("dp", "tensor")),
            P(None, "dp", "tensor"),
            P(None, "dp", "tensor"),
            P("dp"),
            P(("dp", "tensor")),
            P(("dp", "tensor")),
            P(("dp", "tensor")),
            P("dp", "tensor"),
            P("dp", "tensor"),
            P("dp", "tensor"),
        ),
        check_vma=False,
    )
```

profile of v0, /device:TPU:4, one launch (start us, length us, event | category | flops | bytes accessed | tf_op | source)
XLA Modules:
  0.0 515.0 jit_solution(1465619128677415151)
XLA Ops:
  7.2 0.0 reduce-scatter.3.cloned.1.call-start
  7.2 0.7 compare_select_fusion.1
  8.0 0.7 compare_select_fusion.2
  8.6 0.8 select_reduce_fusion.2
  9.5 0.8 select_reduce_fusion.1
  10.3 0.1 pad_add_fusion
  10.4 0.1 select_reduce_fusion
  10.5 0.3 copy-done.11
  10.8 0.1 fusion.4
  10.9 4.2 add_convert_fusion.3
  15.1 0.9 reshape.74
  16.0 7.5 %add_convert_fusion.2 = (bf16[24,49152]{1,0:T(8,128)(2,1)}, f32[24,49152]{1,0:T(8,128)}) fusion(f32[24,49152]{1,0:T(8,128)} %param.18, f32[24,49152]{1,0:T(8,128)} %param.19), kind=kLoop, calls=%fused_computation.12 | loop fusion | flops 5898240 | bytes 16515072 | tf_op jit(solution)/shard_map/convert_element_type | solution.py:20
  23.5 3.5 reshape.75
  27.0 5.3 %fusion = bf16[56,2,12,2048]{3,1,2,0:T(2,128)(2,1)} fusion(bf16[32,2,12,768]{3,1,2,0:T(2,128)(2,1)S(1)} %bitcast.28, bf16[24,2,12,2048]{3,1,2,0:T(2,128)(2,1)S(1)} %bitcast.26), kind=kLoop, calls=%fused_computation.7 | loop fusion | flops 16515072 | bytes 9043968 | tf_op jit(solution)/shard_map/concatenate | solution.py:88
  32.3 17.6 %gather_fusion = bf16[64,2,12,2048]{3,1,2,0:T(2,128)(2,1)} fusion(bf16[56,2,12,2048]{3,1,2,0:T(2,128)(2,1)} %fusion, s32[1024]{0:T(1024)S(1)} %pad_clamp_fusion.2), kind=kCustom, calls=%fused_computation | custom fusion | bytes 12583168 | tf_op jit(solution)/shard_map/gather | solution.py:43
  49.9 9.4 %copy.29 = bf16[64,2,12,2048]{3,2,1,0:T(8,128)(2,1)} copy(bf16[64,2,12,2048]{3,1,2,0:T(2,128)(2,1)} %gather_fusion) | data formatting | bytes 12582912 | tf_op jit(solution)/shard_map/gather | solution.py:43
  59.3 0.1 broadcast_in_dim.99
  59.4 0.2 broadcast_in_dim.100
  59.5 7.2 %bitcast_select_fusion = bf16[128,12,2048]{2,1,0:T(8,128)(2,1)} fusion(bf16[64,2,12,2048]{3,2,1,0:T(8,128)(2,1)} %copy.29, pred[128]{0:T(512)(128)(4,1)S(1)} %broadcast_in_dim.100), kind=kLoop, calls=%fused_computation.6 | loop fusion | flops 3145728 | bytes 12583040 | tf_op jit(solution)/shard_map/jit(_where)/select_n | solution.py:43
  66.8 107.0 %all_to_all.14 = bf16[128,12,2048]{2,1,0:T(8,128)(2,1)} all-to-all(bf16[128,12,2048]{2,1,0:T(8,128)(2,1)} %bitcast_select_fusion), channel_id=1, replica_groups=mesh['dp'=64,'tensor'=2] {'dp','tensor'}, dimensions={0} | all-to-all | bytes 12582912 | tf_op jit(solution)/shard_map/all_to_all | solution.py:91
  173.8 10.7 %all_to_all.10 = bf16[1536,2048]{1,0:T(8,128)(2,1)} reshape(bf16[128,12,2048]{2,1,0:T(8,128)(2,1)} %all_to_all.14) | data formatting | bytes 12582912 | tf_op jit(solution)/shard_map/all_to_all | solution.py:91
  184.5 16.2 %fusion.8 = f32[1536,1536]{1,0:T(8,128)} fusion(bf16[1536,2048]{1,0:T(8,128)(2,1)} %all_to_all.10), kind=kOutput, calls=%fused_computation.48 | convolution fusion | flops 9663676416 | bytes 15728640 | tf_op jit(solution)/shard_map/rc,sc->rs/dot_general | solution.py:99
  200.7 0.0 reduce-scatter.3.cloned.1.call-update
  200.7 0.0 all-gather.5.cloned.1.call-start
  200.8 18.6 %reduce-scatter.3.cloned.1.call-done = f32[768,1536]{1,0:T(8,128)} async-done(((f32[1536,1536]{1,0:T(8,128)}), f32[768,1536]{1,0:T(8,128)}) %reduce-scatter.3.cloned.1.call-update) | async-done | bytes 4718608 | tf_op jit(solution)/shard_map/reduce_scatter | solution.py:98
  219.4 4.2 multiply_reduce_fusion
  223.5 3.1 psum.7
  227.3 4.3 divide_convert_fusion.1
  231.6 0.0 all-gather.5.cloned.1.call-update
  231.6 0.0 all-gather.7.cloned.1.call-start
  231.7 18.6 %all-gather.5.cloned.1.call-done = bf16[1536,1536]{1,0:T(8,128)(2,1)} async-done(((bf16[768,1536]{1,0:T(8,128)(2,1)}), bf16[1536,1536]{1,0:T(8,128)(2,1)}) %all-gather.5.cloned.1.call-update) | async-done | bytes 4718608 | tf_op jit(solution)/shard_map/all_gather | solution.py:113
  250.3 9.1 %add_convert_fusion.1 = bf16[768,1536]{1,0:T(8,128)(2,1)} fusion(bf16[768,1536]{1,0:T(8,128)(2,1)} %divide_convert_fusion.1, bf16[1536,1536]{1,0:T(8,128)(2,1)} %all-gather.5.cloned.1.call-done), kind=kOutput, calls=%fused_computation.9 | convolution fusion | flops 3629776896 | bytes 9437184 | tf_op jit(solution)/shard_map/dot_general | solution.py:111
  259.4 0.0 all-gather.7.cloned.1.call-update
  259.4 0.2 reduce-scatter.5.cloned.1.call-start
  259.7 18.4 %all-gather.7.cloned.1.call-done = bf16[1536,1536]{1,0:T(8,128)(2,1)} async-done(((bf16[768,1536]{1,0:T(8,128)(2,1)}), bf16[1536,1536]{1,0:T(8,128)(2,1)}) %all-gather.7.cloned.1.call-update) | async-done | bytes 4718608 | tf_op jit(solution)/shard_map/all_gather | solution.py:120
  278.1 14.9 %divide_convert_fusion = bf16[1536,2048]{1,0:T(8,128)(2,1)S(1)} fusion(bf16[1536,2048]{1,0:T(8,128)(2,1)} %all_to_all.10, bf16[1536,1536]{1,0:T(8,128)(2,1)} %all-gather.7.cloned.1.call-done, f32[]{:T(128)S(6)} %sqrt.13), kind=kOutput, calls=%fused_computation.5 | convolution fusion | flops 9679405056 | bytes 17301508 | tf_op jit(solution)/shard_map/dot_general | solution.py:119
  293.0 2.7 copy-done.13
  295.6 12.7 %fusion.9 = f32[1536,1536]{1,0:T(8,128)} fusion(bf16[1536,2048]{1,0:T(8,128)(2,1)S(1)} %divide_convert_fusion), kind=kOutput, calls=%fused_computation.49 | convolution fusion | flops 9663676416 | bytes 15728640 | tf_op jit(solution)/shard_map/rc,sc->rs/dot_general | solution.py:99
  308.4 0.0 reduce-scatter.5.cloned.1.call-update
  308.4 0.0 all-gather.9.cloned.1.call-start
  308.4 22.0 %reduce-scatter.5.cloned.1.call-done = f32[768,1536]{1,0:T(8,128)} async-done(((f32[1536,1536]{1,0:T(8,128)}), f32[768,1536]{1,0:T(8,128)}) %reduce-scatter.5.cloned.1.call-update) | async-done | bytes 4718608 | tf_op jit(solution)/shard_map/reduce_scatter | solution.py:98
  330.4 4.0 convert_element_type.49
  334.4 0.0 all-gather.9.cloned.1.call-update
  334.5 0.0 copy-start.12
  334.5 0.3 all-gather.11.cloned.1.call-start
  334.7 18.5 %all-gather.9.cloned.1.call-done = bf16[1536,1536]{1,0:T(8,128)(2,1)} async-done(((bf16[768,1536]{1,0:T(8,128)(2,1)}), bf16[1536,1536]{1,0:T(8,128)(2,1)}) %all-gather.9.cloned.1.call-update) | async-done | bytes 4718608 | tf_op jit(solution)/shard_map/all_gather | solution.py:113
  353.2 9.1 %add_convert_fusion = bf16[768,1536]{1,0:T(8,128)(2,1)} fusion(bf16[768,1536]{1,0:T(8,128)(2,1)} %convert_element_type.49, bf16[1536,1536]{1,0:T(8,128)(2,1)} %all-gather.9.cloned.1.call-done), kind=kOutput, calls=%fused_computation.8 | convolution fusion | flops 3629776896 | bytes 9437184 | tf_op jit(solution)/shard_map/dot_general | solution.py:111
  362.3 0.0 all-gather.11.cloned.1.call-update
  362.3 0.6 compare_reduce_fusion.1
  363.6 17.4 %all-gather.11.cloned.1.call-done = bf16[1536,1536]{1,0:T(8,128)(2,1)} async-done(((bf16[768,1536]{1,0:T(8,128)(2,1)}), bf16[1536,1536]{1,0:T(8,128)(2,1)}) %all-gather.11.cloned.1.call-update) | async-done | bytes 4718608 | tf_op jit(solution)/shard_map/all_gather | solution.py:120
  380.9 16.6 %multiply_convert_fusion = bf16[1536,2048]{1,0:T(8,128)(2,1)} fusion(bf16[1536,2048]{1,0:T(8,128)(2,1)} %copy-done.13, bf16[1536,1536]{1,0:T(8,128)(2,1)} %all-gather.11.cloned.1.call-done, f32[]{:T(128)S(6)} %select_n.54), kind=kOutput, calls=%fused_computation.4 | convolution fusion | flops 9679405056 | bytes 17301508 | tf_op jit(solution)/shard_map/dot_general | solution.py:119
  397.6 0.0 copy-start.5
  397.6 0.0 copy-start.6
  397.6 0.0 copy-start.1
  397.6 0.0 copy-start.2
  397.6 10.7 %all-to-all-start.1 = ((bf16[64,24,2048]{2,1,0:T(8,128)(2,1)}), bf16[64,24,2048]{2,1,0:T(8,128)(2,1)}, u32[]{:S(2)}, u32[]{:S(2)}) async-start(bf16[64,24,2048]{2,1,0:T(8,128)(2,1)} %bitcast.27), calls=%async_computation.3 | async-start | bytes 12582912 | tf_op jit(solution)/shard_map/all_to_all | solution.py:129
  408.4 0.6 compare_reduce_fusion
  410.4 0.1 convert_reduce_fusion
  410.5 0.6 multiply_add_fusion.3
  411.1 1.4 fusion.3
  412.6 84.5 %all-to-all-done.1 = bf16[64,24,2048]{2,1,0:T(8,128)(2,1)} async-done(((bf16[64,24,2048]{2,1,0:T(8,128)(2,1)}), bf16[64,24,2048]{2,1,0:T(8,128)(2,1)}, u32[]{:S(2)}, u32[]{:S(2)}) %all-to-all-start.1) | async-done | bytes 6291488 | tf_op jit(solution)/shard_map/all_to_all | solution.py:129
  497.1 3.5 gather_fusion.1
  500.7 1.1 slice.28
  501.8 5.0 gather_fusion.2
  (28 shorter events, 0.1 us)
Async XLA Ops:
  7.2 212.2 %reduce-scatter.3.cloned.1.call-start = ((), (), s32[]{:S(2)}) async-start(), calls=%async_computation.4 | async-start | bytes 14155776 | tf_op jit(solution)/shard_map/reduce_scatter | solution.py:98
  9.4 1.0 copy-start.9
  10.3 0.5 copy-start.11
  200.7 49.6 %all-gather.5.cloned.1.call-start = ((), (), s32[]{:S(2)}) async-start(), calls=%async_computation.5 | async-start | bytes 7077888 | tf_op jit(solution)/shard_map/all_gather | solution.py:113
  231.6 46.4 %all-gather.7.cloned.1.call-start = ((), (), s32[]{:S(2)}) async-start(), calls=%async_computation.6 | async-start | bytes 7077888 | tf_op jit(solution)/shard_map/all_gather | solution.py:120
  259.4 71.0 %reduce-scatter.5.cloned.1.call-start = ((), (), s32[]{:S(2)}) async-start(), calls=%async_computation.7 | async-start | bytes 14155776 | tf_op jit(solution)/shard_map/reduce_scatter | solution.py:98
  293.0 2.7 copy-start.13
  308.4 44.8 %all-gather.9.cloned.1.call-start = ((), (), s32[]{:S(2)}) async-start(), calls=%async_computation.8 | async-start | bytes 7077888 | tf_op jit(solution)/shard_map/all_gather | solution.py:113
  334.5 27.8 %copy-start.12 = (s32[32]{0:T(128)S(1)}, s32[32]{0:T(128)}, u32[]{:S(2)}) copy-start(s32[32]{0:T(128)} %copy-done.11) | copy-start | bytes 388
  334.5 46.5 %all-gather.11.cloned.1.call-start = ((), (), s32[]{:S(2)}) async-start(), calls=%async_computation.9 | async-start | bytes 7077888 | tf_op jit(solution)/shard_map/all_gather | solution.py:120
  397.5 10.8 %copy-start.10 = (s32[24]{0:T(128)S(1)}, s32[24]{0:T(128)}, u32[]{:S(2)}) copy-start(s32[24]{0:T(128)} %copy-done.9) | copy-start | bytes 292
  397.6 12.8 %copy-start.8 = (s32[16,2]{0,1:T(2,128)S(1)}, s32[16,2]{0,1:T(2,128)}, u32[]{:S(2)}) copy-start(s32[16,2]{0,1:T(2,128)} %param.31) | copy-start | bytes 388
  397.6 12.9 %copy-start.4 = (f32[1344]{0:T(1024)S(1)}, f32[1344]{0:T(1024)}, u32[]{:S(2)}) copy-start(f32[1344]{0:T(1024)} %param.23) | copy-start | bytes 16132
  397.6 12.9 %copy-start.5 = (f32[1344]{0:T(1024)S(1)}, f32[1344]{0:T(1024)}, u32[]{:S(2)}) copy-start(f32[1344]{0:T(1024)} %param.24) | copy-start | bytes 16132
  397.6 12.9 %copy-start.6 = (f32[1344]{0:T(1024)S(1)}, f32[1344]{0:T(1024)}, u32[]{:S(2)}) copy-start(f32[1344]{0:T(1024)} %param.25) | copy-start | bytes 16132
  397.6 12.9 %copy-start.7 = (f32[1344]{0:T(1024)S(1)}, f32[1344]{0:T(1024)}, u32[]{:S(2)}) copy-start(f32[1344]{0:T(1024)} %param.26) | copy-start | bytes 16132
  397.6 13.5 %copy-start = (f32[128,768]{1,0:T(8,128)S(1)}, f32[128,768]{1,0:T(8,128)}, u32[]{:S(2)}) copy-start(f32[128,768]{1,0:T(8,128)} %param.30) | copy-start | bytes 1179652
  397.6 13.5 %copy-start.1 = (f32[128,768]{1,0:T(8,128)S(1)}, f32[128,768]{1,0:T(8,128)}, u32[]{:S(2)}) copy-start(f32[128,768]{1,0:T(8,128)} %param.28) | copy-start | bytes 1179652
  397.6 13.5 %copy-start.2 = (f32[128,768]{1,0:T(8,128)S(1)}, f32[128,768]{1,0:T(8,128)}, u32[]{:S(2)}) copy-start(f32[128,768]{1,0:T(8,128)} %param.27) | copy-start | bytes 1179652
  397.6 13.5 %copy-start.3 = (f32[128,768]{1,0:T(8,128)S(1)}, f32[128,768]{1,0:T(8,128)}, u32[]{:S(2)}) copy-start(f32[128,768]{1,0:T(8,128)} %param.29) | copy-start | bytes 1179652
  397.6 99.5 %all-to-all-start.1 = ((bf16[64,24,2048]{2,1,0:T(8,128)(2,1)}), bf16[64,24,2048]{2,1,0:T(8,128)(2,1)}, u32[]{:S(2)}, u32[]{:S(2)}) async-start(bf16[64,24,2048]{2,1,0:T(8,128)(2,1)} %bitcast.27), calls=%async_computation.3 | async-start | bytes 12582912 | tf_op jit(solution)/shard_map/all_to_all | solution.py:129
Sparse Core Ops, SparseCore 0:
  200.8 18.4 reduce-scatter.2
  231.8 18.5 all-gather.4
  259.5 18.4 all-gather.6
  308.5 21.8 reduce-scatter.4
  334.6 18.5 all-gather.8
  362.4 18.4 all-gather.10
where the time goes:
time: 524 us; the launch traced here: 515 us
  waiting for transfers between devices  198 us (38%)
  blocking collectives  110 us (21%)
  matrix products  78.6 us (15%)
  local copies, waits for them, and re-layouts  55 us (10%)
  other arithmetic  43.4 us (8%)
  between operations  18.5 us (4%)
  starting transfers between devices  11.3 us (2%)
    all_to_all x1, blocking collectives, local(): lax.all_to_all(outgoing.reshape(D, slot_width), ('dp', 'tensor'), split_a...  107 us
    all_to_all x1, waiting for transfers between devices, local(): lax.all_to_all(iterate.reshape(wide_count, D // wide_count, slot_width),...  84.5 us
    reduce_scatter x2, waiting for transfers between devices, local(): lax.psum_scatter(jnp.einsum('rc,sc->rs', current, current, preferred_elem...  40.6 us
    all_gather x2, waiting for transfers between devices, local(): lax.all_gather(normed_part, 'tensor', axis=0, tiled=True)  37.1 us
    all_gather x2, waiting for transfers between devices, local(): lax.all_gather(polynomial, 'tensor', axis=0, tiled=True)  35.7 us
    dot_general x2, matrix products, local(): jnp.dot(lax.all_gather(polynomial, 'tensor', axis=0, tiled=True), current...  31.5 us
    dot_general x2, matrix products, local(): jnp.einsum('rc,sc->rs', current, current, preferred_element_type=jnp.floa...  29 us
    gather x2, local copies, waits for them, and re-layouts, select_pieces(): pieces[chosen]  27 us
  transfers between devices with their start and end apart: 7, of which 7 were waited for; matrix products, arithmetic and copies ran while one was open for 1% of the time, Pallas kernels for 0%

commit v1 on v0

--- a/solution.py
+++ b/solution.py
@@ -13,6 +13,11 @@
 MOMENTUM = 0.95
 BIAS_FIRST = 1.0 - 0.9**10
 BIAS_SECOND = 1.0 - 0.95**10
+
+
+def gather_by_exchange(x, axis, dim):
+    copies = jnp.concatenate([x] * lax.axis_size(axis), axis=dim)
+    return lax.all_to_all(copies, axis, dim, dim, tiled=True)
 
 
 def momentum_terms(gradient, state):
@@ -110,7 +115,7 @@
         normed_part = (gram_part / gram_scale).astype(jnp.bfloat16)
         squared = jnp.dot(
             normed_part,
-            lax.all_gather(normed_part, "tensor", axis=0, tiled=True),
+            gather_by_exchange(normed_part, "tensor", 0),
             preferred_element_type=jnp.float32,
         )
         polynomial = (

time: 524 us -> 483 us (0.922); the launches traced: 515 us -> 481 us
  waiting for transfers between devices: 198 us -> 161 us
  blocking collectives: 110 us -> 125 us
  matrix products: 78.6 us -> 70.6 us
    all_gather x2 -> x0, waiting for transfers between devices: 37.1 us -> none  [local(): lax.all_gather(normed_part, 'tensor', axis=0, tiled=True)]
    all_to_all x0 -> x2, blocking collectives: none -> 15.1 us  [gather_by_exchange(): return lax.all_to_all(copies, axis, dim, dim, tiled=True)]
    dot_general x2, matrix products: 18.2 us -> 10.2 us  [local(): jnp.dot(normed_part, gather_by_exchange(normed_part, 'tensor', 0), prefer...]
  transfers between devices with their start and end apart: 7 -> 5, of which waited for: 7 -> 5; matrix products, arithmetic and copies ran while one was open for 1% -> 1% of each run, Pallas kernels for 0% -> 0%
where the time goes in v1:
time: 483 us; the launch traced here: 481 us
  waiting for transfers between devices  161 us (33%)
  blocking collectives  125 us (26%)
  matrix products  70.6 us (15%)
  local copies, waits for them, and re-layouts  55 us (11%)
  other arithmetic  41.3 us (9%)
  between operations  17.9 us (4%)
  starting transfers between devices  11.1 us (2%)
    all_to_all x1, blocking collectives, local(): lax.all_to_all(outgoing.reshape(D, slot_width), ('dp', 'tensor'), split_a...  107 us
    all_to_all x1, waiting for transfers between devices, local(): lax.all_to_all(iterate.reshape(wide_count, D // wide_count, slot_width),...  84.5 us
    reduce_scatter x2, waiting for transfers between devices, local(): lax.psum_scatter(jnp.einsum('rc,sc->rs', current, current, preferred_elem...  40.5 us
    all_gather x2, waiting for transfers between devices, local(): lax.all_gather(polynomial, 'tensor', axis=0, tiled=True)  35.7 us
    dot_general x2, matrix products, local(): jnp.dot(lax.all_gather(polynomial, 'tensor', axis=0, tiled=True), current...  31.5 us
    dot_general x2, matrix products, local(): jnp.einsum('rc,sc->rs', current, current, preferred_element_type=jnp.floa...  29 us
    gather x2, local copies, waits for them, and re-layouts, select_pieces(): pieces[chosen]  27 us
    all_to_all x2, blocking collectives, gather_by_exchange(): return lax.all_to_all(copies, axis, dim, dim, tiled=True)  15.1 us
  transfers between devices with their start and end apart: 5, of which 5 were waited for; matrix products, arithmetic and copies ran while one was open for 1% of the time, Pallas kernels for 0%

profile of v1, /device:TPU:4, one launch (start us, length us, event | category | flops | bytes accessed | tf_op | source)
XLA Modules:
  0.0 481.5 jit_solution(7356289580619887734)
XLA Ops:
  7.2 0.0 reduce-scatter.3.cloned.1.call-start
  7.2 0.7 compare_select_fusion.1
  8.0 0.7 compare_select_fusion.2
  8.6 0.8 select_reduce_fusion.2
  9.5 0.8 select_reduce_fusion.1
  10.3 0.1 pad_add_fusion
  10.4 0.1 select_reduce_fusion
  10.5 0.3 copy-done.11
  10.8 0.1 fusion.4
  10.9 4.2 add_convert_fusion.3
  15.1 0.9 reshape.78
  16.0 7.5 %add_convert_fusion.2 = (bf16[24,49152]{1,0:T(8,128)(2,1)}, f32[24,49152]{1,0:T(8,128)}) fusion(f32[24,49152]{1,0:T(8,128)} %param.18, f32[24,49152]{1,0:T(8,128)} %param.19), kind=kLoop, calls=%fused_computation.14 | loop fusion | flops 5898240 | bytes 16515072 | tf_op jit(solution)/shard_map/convert_element_type | solution.py:25
  23.5 3.5 reshape.79
  27.0 5.3 %fusion = bf16[56,2,12,2048]{3,1,2,0:T(2,128)(2,1)} fusion(bf16[32,2,12,768]{3,1,2,0:T(2,128)(2,1)S(1)} %bitcast.34, bf16[24,2,12,2048]{3,1,2,0:T(2,128)(2,1)S(1)} %bitcast.32), kind=kLoop, calls=%fused_computation.7 | loop fusion | flops 16515072 | bytes 9043968 | tf_op jit(solution)/shard_map/concatenate | solution.py:93
  32.3 17.6 %gather_fusion = bf16[64,2,12,2048]{3,1,2,0:T(2,128)(2,1)} fusion(bf16[56,2,12,2048]{3,1,2,0:T(2,128)(2,1)} %fusion, s32[1024]{0:T(1024)S(1)} %pad_clamp_fusion.2), kind=kCustom, calls=%fused_computation | custom fusion | bytes 12583168 | tf_op jit(solution)/shard_map/gather | solution.py:48
  49.9 9.4 %copy.29 = bf16[64,2,12,2048]{3,2,1,0:T(8,128)(2,1)} copy(bf16[64,2,12,2048]{3,1,2,0:T(2,128)(2,1)} %gather_fusion) | data formatting | bytes 12582912 | tf_op jit(solution)/shard_map/gather | solution.py:48
  59.3 0.1 broadcast_in_dim.99
  59.4 0.2 broadcast_in_dim.100
  59.5 7.2 %bitcast_select_fusion = bf16[128,12,2048]{2,1,0:T(8,128)(2,1)} fusion(bf16[64,2,12,2048]{3,2,1,0:T(8,128)(2,1)} %copy.29, pred[128]{0:T(512)(128)(4,1)S(1)} %broadcast_in_dim.100), kind=kLoop, calls=%fused_computation.6 | loop fusion | flops 3145728 | bytes 12583040 | tf_op jit(solution)/shard_map/jit(_where)/select_n | solution.py:48
  66.7 106.5 %all_to_all.38 = bf16[128,12,2048]{2,1,0:T(8,128)(2,1)} all-to-all(bf16[128,12,2048]{2,1,0:T(8,128)(2,1)} %bitcast_select_fusion), channel_id=1, replica_groups=mesh['dp'=64,'tensor'=2] {'dp','tensor'}, dimensions={0} | all-to-all | bytes 12582912 | tf_op jit(solution)/shard_map/all_to_all | solution.py:96
  173.3 10.7 %all_to_all.26 = bf16[1536,2048]{1,0:T(8,128)(2,1)} reshape(bf16[128,12,2048]{2,1,0:T(8,128)(2,1)} %all_to_all.38) | data formatting | bytes 12582912 | tf_op jit(solution)/shard_map/all_to_all | solution.py:96
  184.0 16.2 %fusion.8 = f32[1536,1536]{1,0:T(8,128)} fusion(bf16[1536,2048]{1,0:T(8,128)(2,1)} %all_to_all.26), kind=kOutput, calls=%fused_computation.50 | convolution fusion | flops 9663676416 | bytes 15728640 | tf_op jit(solution)/shard_map/rc,sc->rs/dot_general | solution.py:104
  200.2 0.0 reduce-scatter.3.cloned.1.call-update
  200.2 0.0 all-gather.3.cloned.1.call-start
  200.3 18.6 %reduce-scatter.3.cloned.1.call-done = f32[768,1536]{1,0:T(8,128)} async-done(((f32[1536,1536]{1,0:T(8,128)}), f32[768,1536]{1,0:T(8,128)}) %reduce-scatter.3.cloned.1.call-update) | async-done | bytes 4718608 | tf_op jit(solution)/shard_map/reduce_scatter | solution.py:103
  218.9 4.2 multiply_reduce_fusion
  223.0 3.1 psum.7
  226.8 2.9 divide_convert_fusion.1
  229.7 0.4 pad_maximum_fusion
  230.1 7.5 %all_to_all.39 = bf16[2,768,1536]{2,1,0:T(8,128)(2,1)S(1)} all-to-all(bf16[2,768,1536]{2,1,0:T(8,128)(2,1)S(1)} %bitcast.30), channel_id=1, replica_groups=mesh['dp'=64,'tensor'=2] {'tensor'}, dimensions={0} | all-to-all | bytes 9437184 | tf_op jit(solution)/shard_map/all_to_all | solution.py:20
  237.6 5.1 %add_convert_fusion.1 = bf16[768,1536]{1,0:T(8,128)(2,1)} fusion(bf16[768,1536]{1,0:T(8,128)(2,1)S(1)} %divide_convert_fusion.1, bf16[1536,1536]{1,0:T(8,128)(2,1)S(1)} %bitcast.35), kind=kOutput, calls=%fused_computation.11 | convolution fusion | flops 3629776896 | bytes 9437184 | tf_op jit(solution)/shard_map/dot_general | solution.py:116
  242.7 0.0 all-gather.3.cloned.1.call-update
  242.7 0.3 reduce-scatter.5.cloned.1.call-start
  243.0 18.3 %all-gather.3.cloned.1.call-done = bf16[1536,1536]{1,0:T(8,128)(2,1)} async-done(((bf16[768,1536]{1,0:T(8,128)(2,1)}), bf16[1536,1536]{1,0:T(8,128)(2,1)}) %all-gather.3.cloned.1.call-update) | async-done | bytes 4718608 | tf_op jit(solution)/shard_map/all_gather | solution.py:125
  261.3 14.9 %divide_convert_fusion = bf16[1536,2048]{1,0:T(8,128)(2,1)S(1)} fusion(bf16[1536,2048]{1,0:T(8,128)(2,1)} %all_to_all.26, bf16[1536,1536]{1,0:T(8,128)(2,1)} %all-gather.3.cloned.1.call-done, f32[]{:T(128)S(6)} %sqrt.13), kind=kOutput, calls=%fused_computation.5 | convolution fusion | flops 9679405056 | bytes 17301508 | tf_op jit(solution)/shard_map/dot_general | solution.py:124
  276.2 2.7 copy-done.13
  278.9 12.7 %fusion.9 = f32[1536,1536]{1,0:T(8,128)} fusion(bf16[1536,2048]{1,0:T(8,128)(2,1)S(1)} %divide_convert_fusion), kind=kOutput, calls=%fused_computation.51 | convolution fusion | flops 9663676416 | bytes 15728640 | tf_op jit(solution)/shard_map/rc,sc->rs/dot_general | solution.py:104
  291.7 0.0 reduce-scatter.5.cloned.1.call-update
  291.7 0.0 all-gather.5.cloned.1.call-start
  291.7 22.0 %reduce-scatter.5.cloned.1.call-done = f32[768,1536]{1,0:T(8,128)} async-done(((f32[1536,1536]{1,0:T(8,128)}), f32[768,1536]{1,0:T(8,128)}) %reduce-scatter.5.cloned.1.call-update) | async-done | bytes 4718608 | tf_op jit(solution)/shard_map/reduce_scatter | solution.py:103
  313.7 2.6 convert_element_type.49
  316.3 0.4 pad_maximum_fusion.1
  316.7 7.5 %all_to_all.40 = bf16[2,768,1536]{2,1,0:T(8,128)(2,1)S(1)} all-to-all(bf16[2,768,1536]{2,1,0:T(8,128)(2,1)S(1)} %bitcast.31), channel_id=1, replica_groups=mesh['dp'=64,'tensor'=2] {'tensor'}, dimensions={0} | all-to-all | bytes 9437184 | tf_op jit(solution)/shard_map/all_to_all | solution.py:20
  324.2 5.1 %add_convert_fusion = bf16[768,1536]{1,0:T(8,128)(2,1)} fusion(bf16[768,1536]{1,0:T(8,128)(2,1)S(1)} %convert_element_type.49, bf16[1536,1536]{1,0:T(8,128)(2,1)S(1)} %bitcast.36), kind=kOutput, calls=%fused_computation.10 | convolution fusion | flops 3629776896 | bytes 9437184 | tf_op jit(solution)/shard_map/dot_general | solution.py:116
  329.3 0.0 all-gather.5.cloned.1.call-update
  329.4 0.6 compare_reduce_fusion.1
  330.7 17.3 %all-gather.5.cloned.1.call-done = bf16[1536,1536]{1,0:T(8,128)(2,1)} async-done(((bf16[768,1536]{1,0:T(8,128)(2,1)}), bf16[1536,1536]{1,0:T(8,128)(2,1)}) %all-gather.5.cloned.1.call-update) | async-done | bytes 4718608 | tf_op jit(solution)/shard_map/all_gather | solution.py:125
  348.0 16.6 %multiply_convert_fusion = bf16[1536,2048]{1,0:T(8,128)(2,1)} fusion(bf16[1536,2048]{1,0:T(8,128)(2,1)} %copy-done.13, bf16[1536,1536]{1,0:T(8,128)(2,1)} %all-gather.5.cloned.1.call-done, f32[]{:T(128)S(6)} %select_n.54), kind=kOutput, calls=%fused_computation.4 | convolution fusion | flops 9679405056 | bytes 17301508 | tf_op jit(solution)/shard_map/dot_general | solution.py:124
  364.6 0.0 copy-start.5
  364.6 0.0 copy-start.6
  364.6 0.0 copy-start.7
  364.6 0.0 copy-start
  364.7 0.0 copy-start.1
  364.7 0.0 copy-start.2
  364.7 0.0 copy-start.3
  364.7 10.7 %all-to-all-start.3 = ((bf16[64,24,2048]{2,1,0:T(8,128)(2,1)}), bf16[64,24,2048]{2,1,0:T(8,128)(2,1)}, u32[]{:S(2)}, u32[]{:S(2)}) async-start(bf16[64,24,2048]{2,1,0:T(8,128)(2,1)} %bitcast.33), calls=%async_computation.5 | async-start | bytes 12582912 | tf_op jit(solution)/shard_map/all_to_all | solution.py:134
  375.4 0.6 compare_reduce_fusion
  377.4 0.1 convert_reduce_fusion
  377.5 0.6 multiply_add_fusion.3
  378.2 1.4 fusion.3
  379.7 84.5 %all-to-all-done.3 = bf16[64,24,2048]{2,1,0:T(8,128)(2,1)} async-done(((bf16[64,24,2048]{2,1,0:T(8,128)(2,1)}), bf16[64,24,2048]{2,1,0:T(8,128)(2,1)}, u32[]{:S(2)}, u32[]{:S(2)}) %all-to-all-start.3) | async-done | bytes 6291488 | tf_op jit(solution)/shard_map/all_to_all | solution.py:134
  464.2 3.5 gather_fusion.1
  467.7 1.1 slice.28
  468.8 5.0 %gather_fusion.2 = bf16[24,24,2048]{2,1,0:T(8,128)(2,1)} fusion(bf16[64,24,2048]{2,1,0:T(8,128)(2,1)} %all-to-all-done.3, s32[1024]{0:T(1024)S(1)} %pad_clamp_fusion), kind=kCustom, calls=%fused_computation.2 | custom fusion | bytes 4718688 | tf_op jit(solution)/shard_map/gather | solution.py:142
  (26 shorter events, 0.1 us)
Async XLA Ops:
  7.2 211.7 %reduce-scatter.3.cloned.1.call-start = ((), (), s32[]{:S(2)}) async-start(), calls=%async_computation.6 | async-start | bytes 14155776 | tf_op jit(solution)/shard_map/reduce_scatter | solution.py:103
  9.4 1.0 copy-start.9
  10.3 0.5 copy-start.11
  200.2 61.1 %all-gather.3.cloned.1.call-start = ((), (), s32[]{:S(2)}) async-start(), calls=%async_computation.7 | async-start | bytes 7077888 | tf_op jit(solution)/shard_map/all_gather | solution.py:125
  242.7 71.0 %reduce-scatter.5.cloned.1.call-start = ((), (), s32[]{:S(2)}) async-start(), calls=%async_computation.8 | async-start | bytes 14155776 | tf_op jit(solution)/shard_map/reduce_scatter | solution.py:103
  276.2 2.7 copy-start.13
  291.7 56.3 %all-gather.5.cloned.1.call-start = ((), (), s32[]{:S(2)}) async-start(), calls=%async_computation.9 | async-start | bytes 7077888 | tf_op jit(solution)/shard_map/all_gather | solution.py:125
  324.2 5.1 %copy-start.12 = (s32[32]{0:T(128)S(1)}, s32[32]{0:T(128)}, u32[]{:S(2)}) copy-start(s32[32]{0:T(128)} %copy-done.11) | copy-start | bytes 388
  364.6 10.8 %copy-start.10 = (s32[24]{0:T(128)S(1)}, s32[24]{0:T(128)}, u32[]{:S(2)}) copy-start(s32[24]{0:T(128)} %copy-done.9) | copy-start | bytes 292
  364.6 12.8 %copy-start.8 = (s32[16,2]{0,1:T(2,128)S(1)}, s32[16,2]{0,1:T(2,128)}, u32[]{:S(2)}) copy-start(s32[16,2]{0,1:T(2,128)} %param.31) | copy-start | bytes 388
  364.6 12.9 %copy-start.4 = (f32[1344]{0:T(1024)S(1)}, f32[1344]{0:T(1024)}, u32[]{:S(2)}) copy-start(f32[1344]{0:T(1024)} %param.23) | copy-start | bytes 16132
  364.6 12.9 %copy-start.5 = (f32[1344]{0:T(1024)S(1)}, f32[1344]{0:T(1024)}, u32[]{:S(2)}) copy-start(f32[1344]{0:T(1024)} %param.24) | copy-start | bytes 16132
  364.6 12.9 %copy-start.6 = (f32[1344]{0:T(1024)S(1)}, f32[1344]{0:T(1024)}, u32[]{:S(2)}) copy-start(f32[1344]{0:T(1024)} %param.25) | copy-start | bytes 16132
  364.6 12.9 %copy-start.7 = (f32[1344]{0:T(1024)S(1)}, f32[1344]{0:T(1024)}, u32[]{:S(2)}) copy-start(f32[1344]{0:T(1024)} %param.26) | copy-start | bytes 16132
  364.6 13.5 %copy-start = (f32[128,768]{1,0:T(8,128)S(1)}, f32[128,768]{1,0:T(8,128)}, u32[]{:S(2)}) copy-start(f32[128,768]{1,0:T(8,128)} %param.30) | copy-start | bytes 1179652
  364.7 13.5 %copy-start.1 = (f32[128,768]{1,0:T(8,128)S(1)}, f32[128,768]{1,0:T(8,128)}, u32[]{:S(2)}) copy-start(f32[128,768]{1,0:T(8,128)} %param.28) | copy-start | bytes 1179652
  364.7 13.5 %copy-start.2 = (f32[128,768]{1,0:T(8,128)S(1)}, f32[128,768]{1,0:T(8,128)}, u32[]{:S(2)}) copy-start(f32[128,768]{1,0:T(8,128)} %param.27) | copy-start | bytes 1179652
  364.7 13.5 %copy-start.3 = (f32[128,768]{1,0:T(8,128)S(1)}, f32[128,768]{1,0:T(8,128)}, u32[]{:S(2)}) copy-start(f32[128,768]{1,0:T(8,128)} %param.29) | copy-start | bytes 1179652
  364.7 99.5 %all-to-all-start.3 = ((bf16[64,24,2048]{2,1,0:T(8,128)(2,1)}), bf16[64,24,2048]{2,1,0:T(8,128)(2,1)}, u32[]{:S(2)}, u32[]{:S(2)}) async-start(bf16[64,24,2048]{2,1,0:T(8,128)(2,1)} %bitcast.33), calls=%async_computation.5 | async-start | bytes 12582912 | tf_op jit(solution)/shard_map/all_to_all | solution.py:134
Sparse Core Ops, SparseCore 0:
  200.4 18.4 reduce-scatter.2
  242.8 18.4 all-gather.2
  291.8 21.8 reduce-scatter.4
  329.5 18.4 all-gather.4
